TPU v7x, 32 devices: a whole 2x2x4 slice. The times are simulated.
32 devices in a mesh: row: 8 (over z, core), col: 4 (over y, x).
Axes of the slice: x: 2, y: 2, z: 4, core: 2. Of those that a mesh axis runs over, the one named last changes fastest.
Arguments:
- inputs: bfloat16 [2, 64, 8192], P(None, None, 'col'), may hold values from -6 to 6
- w_input: bfloat16 [2, 4, 8192, 8192], P(None, None, 'row', 'col'), may hold values from -0.0625 to 0.0625
- w_recur: bfloat16 [2, 4, 8192, 8192], P(None, None, 'row', 'col'), may hold values from -0.0625 to 0.0625
- gate_bias: float32 [2, 4, 8192], P(None, None, 'row'), may hold values from -1 to 2
- hidden_init: bfloat16 [2, 64, 8192], P(None, None, ('row', 'col')), may hold values from -3 to 3
- cell_init: float32 [2, 64, 8192], P(None, None, ('row', 'col')), may hold values from -6 to 6
Outputs:
- top_hidden: bfloat16 [2, 64, 8192], P(None, None, ('row', 'col'))
- final_hidden: bfloat16 [2, 64, 8192], P(None, None, ('row', 'col'))
- final_cell: float32 [2, 64, 8192], P(None, None, ('row', 'col'))
All inputs are finite; a program needn't handle non-finite values.
Results may differ from a plain program's by a relative error of at most 0.009.
Values may be sent and summed in bfloat16 or wider, within the bound.
A program may use at most 128 MiB of HBM per device.

v0:
```python
import jax
import jax.numpy as jnp
from jax import lax
from jax.sharding import PartitionSpec as P


def lstm_cell(gate_total, cell_state):
    input_gate = jax.nn.sigmoid(gate_total[:, 0])
    forget_gate = jax.nn.sigmoid(gate_total[:, 1])
    candidate = jnp.tanh(gate_total[:, 2])
    output_gate = jax.nn.sigmoid(gate_total[:, 3])
    cell_state = forget_gate * cell_state + input_gate * candidate
    return (cell_state, (output_gate * jnp.tanh(cell_state)).astype(jnp.bfloat16))


def body(inputs, w_input, w_recur, gate_bias, hidden_init, cell_init):
    col_place = lax.axis_index("col")
    unit_width = hidden_init.shape[2]
    layers = w_input.shape[0]
    block_rows = w_input.shape[2]

    def project(vectors, weight):
        leading = vectors.shape[:-1]
        flattened = vectors.reshape(-1, vectors.shape[-1])
        result = lax.dot_general(
            flattened,
            weight.reshape(-1, weight.shape[-1]),
            (((1,), (1,)), ((), ())),
            preferred_element_type=jnp.float32,
        )
        return result.reshape(leading + (4, block_rows))

    def to_columns(owned):
        return lax.all_gather(owned, "row", axis=1, tiled=True)

    def gate_sums(partial_value, layer):
        bias_part = lax.dynamic_slice_in_dim(
            gate_bias[layer], col_place * unit_width, unit_width, 1
        )
        return (
            lax.psum_scatter(
                partial_value.astype(jnp.bfloat16), "col", scatter_dimension=2, tiled=True
            ).astype(jnp.float32)
            + bias_part[None]
        )

    def step_terms(layer, step_item):
        return project(step_item, w_input[layer])

    def advance(layer, lower_part, columns, cell_state):
        partial_value = lower_part + project(columns, w_recur[layer])
        cell_state, hidden = lstm_cell(gate_sums(partial_value, layer), cell_state)
        return (hidden, to_columns(hidden), cell_state)

    start_columns = tuple((to_columns(hidden_init[layer]) for layer in range(layers)))
    start_owned = tuple((hidden_init[layer] for layer in range(layers)))
    start_state = tuple((cell_init[layer] for layer in range(layers)))

    def advance_time(carried, step_item):
        owned_all, columns_all, cells_all = carried
        next_owned, next_columns, next_cells = ([], [], [])
        lower_part = step_terms(0, step_item)
        for layer in range(layers):
            if layer > 0:
                lower_part = project(next_columns[layer - 1], w_input[layer])
            owned, columns, cell_state = advance(
                layer, lower_part, columns_all[layer], cells_all[layer]
            )
            next_owned.append(owned)
            next_columns.append(columns)
            next_cells.append(cell_state)
        return ((tuple(next_owned), tuple(next_columns), tuple(next_cells)), next_owned[-1])

    carried, top_hidden = lax.scan(advance_time, (start_owned, start_columns, start_state), inputs)
    final_owned, final_columns, final_cells = carried
    final_hidden = jnp.stack(final_owned)
    final_cell = jnp.stack(final_cells)
    return (top_hidden, final_hidden, final_cell)


def solution(mesh):
    in_specs = (
        P(None, None, "col"),
        P(None, None, "row", "col"),
        P(None, None, "row", "col"),
        P(None, None, "row"),
        P(None, None, ("row", "col")),
        P(None, None, ("row", "col")),
    )
    out_specs = (
        P(None, None, ("row", "col")),
        P(None, None, ("row", "col")),
        P(None, None, ("row", "col")),
    )
    return jax.shard_map(body, mesh=mesh, in_specs=in_specs, out_specs=out_specs, check_vma=False)
```

profile of v0, /device:TPU:0, one launch (start us, length us, event | category | flops | bytes accessed | tf_op | source)
XLA Modules:
  0.0 273.1 jit_solution(4128591278328970384)
XLA Ops:
  7.2 0.7 fusion.68
  7.9 1.4 fusion.67
  9.3 15.9 %all-gather = bf16[1,64,2048]{2,1,0:T(8,128)(2,1)S(1)} all-gather(bf16[1,64,256]{2,1,0:T(8,128)(2,1)S(1)} %get-tuple-element.197), channel_id=2, replica_groups=mesh['row'=8,'col'=4] {'row'}, dimensions={2}, use_global_device_ids=true | all-gather | bytes 294912 | tf_op jit(solution)/shard_map/all_gather | solution.py:34
  25.2 14.2 %all-gather.1 = bf16[1,64,2048]{2,1,0:T(8,128)(2,1)S(1)} all-gather(bf16[1,64,256]{2,1,0:T(8,128)(2,1)S(1)} %get-tuple-element.194), channel_id=3, replica_groups=mesh['row'=8,'col'=4] {'row'}, dimensions={2}, use_global_device_ids=true | all-gather | bytes 294912 | tf_op jit(solution)/shard_map/all_gather | solution.py:34
  39.4 0.9 slice_bitcast_fusion
  40.3 224.2 %while.24 = (s32[]{:T(128)}, bf16[64,256]{1,0:T(8,128)(2,1)}, bf16[64,256]{1,0:T(8,128)(2,1)}, bf16[64,2048]{1,0:T(8,128)(2,1)S(1)}, bf16[64,2048]{1,0:T(8,128)(...) while((s32[]{:T(128)}, bf16[64,256]{1,0:T(8,128)(2,1)}, ...), condition=%wide.region_3.4_spmd, body=%wide.region_0.3_spmd.sunk | while | flops 4296736768 | bytes 79864096 | solution.py:74
  40.3 0.0 reduce-scatter.3.cloned.1.call-start
  40.4 8.7 %fusion.90 = f32[64,4,1024]{2,0,1:T(8,128)S(1)} fusion(bf16[2,4,1024,2048]{3,2,1,0:T(8,128)(2,1)} %get-tuple-element.325, bf16[64,2048]{1,0:T(8,128)(2,1)S(1)} %get-tuple-element.304), kind=kOutput, calls=%fused_computation.4.clone.1 | convolution fusion | flops 1073741824 | bytes 18087936 | tf_op jit(solution)/shard_map/while/body/eval_jaxpr/dot_general | solution.py:25
  49.1 11.9 %fusion.91 = bf16[64,4,1024]{2,0,1:T(8,128)(2,1)} fusion(f32[64,4,1024]{2,0,1:T(8,128)S(1)} %fusion.90, bf16[2,4,1024,2048]{3,2,1,0:T(8,128)(2,1)} %get-tuple-element.324, bf16[2,64,2048]{2,1,0:T(8,128)(2,1)} %get-tuple-element.323, s32[]{:T(128)S(6)} %copy.18), kind=kOutput, calls=%fused_computation.15.clone.1 | convolution fusion | flops 1074266112 | bytes 18612228 | tf_op jit(solution)/shard_map/while/body/eval_jaxpr/dot_general | solution.py:25
  61.0 0.0 reduce-scatter.3.cloned.1.call-update
  61.0 0.0 reduce-scatter.5.cloned.1.call-start
  61.1 8.7 %fusion.93 = f32[64,4,1024]{2,0,1:T(8,128)S(1)} fusion(bf16[2,4,1024,2048]{3,2,1,0:T(8,128)(2,1)} %get-tuple-element.325, bf16[64,2048]{1,0:T(8,128)(2,1)S(1)} %get-tuple-element.305), kind=kOutput, calls=%fused_computation.clone.1 | convolution fusion | flops 1073741824 | bytes 18087936 | tf_op jit(solution)/shard_map/while/body/eval_jaxpr/dot_general | solution.py:25
  69.8 17.6 %reduce-scatter.3.cloned.1.call-done = bf16[64,4,256]{2,0,1:T(8,128)(2,1)} async-done(((bf16[64,4,1024]{2,0,1:T(8,128)(2,1)}), bf16[64,4,256]{2,0,1:T(8,128)(2,1)}) %reduce-scatter.3.cloned.1.call-update) | async-done | bytes 131088 | tf_op jit(solution)/shard_map/while/body/eval_jaxpr/reduce_scatter | solution.py:41
  87.4 0.9 convert_add_fusion.4
  88.3 0.1 fusion.92
  88.4 0.0 copy-start
  88.4 14.3 %all_gather.20 = bf16[64,2048]{1,0:T(8,128)(2,1)S(1)} all-gather(bf16[64,256]{1,0:T(8,128)(2,1)S(1)} %get-tuple-element.316), channel_id=1, replica_groups=mesh['row'=8,'col'=4] {'row'}, dimensions={1}, use_global_device_ids=true | all-gather | bytes 294912 | tf_op jit(solution)/shard_map/while/body/eval_jaxpr/all_gather | solution.py:34
  102.7 9.7 %fusion.94 = bf16[64,4,1024]{2,0,1:T(8,128)(2,1)} fusion(f32[64,4,1024]{2,0,1:T(8,128)S(1)} %fusion.93, bf16[2,4,1024,2048]{3,2,1,0:T(8,128)(2,1)} %get-tuple-element.324, bf16[64,2048]{1,0:T(8,128)(2,1)S(1)} %all_gather.20), kind=kOutput, calls=%fused_computation.14.clone.1 | convolution fusion | flops 1074266112 | bytes 18612224 | tf_op jit(solution)/shard_map/while/body/eval_jaxpr/dot_general | solution.py:25
  112.4 0.0 reduce-scatter.5.cloned.1.call-update
  112.4 25.2 %reduce-scatter.5.cloned.1.call-done = bf16[64,4,256]{2,0,1:T(8,128)(2,1)} async-done(((bf16[64,4,1024]{2,0,1:T(8,128)(2,1)}), bf16[64,4,256]{2,0,1:T(8,128)(2,1)}) %reduce-scatter.5.cloned.1.call-update) | async-done | bytes 131088 | tf_op jit(solution)/shard_map/while/body/eval_jaxpr/reduce_scatter | solution.py:41
  137.6 0.9 convert_add_fusion.5
  138.6 0.1 bitcast_dynamic-update-slice_fusion.2
  138.6 0.0 copy-start.1
  138.7 14.3 %all_gather.21 = bf16[64,2048]{1,0:T(8,128)(2,1)S(1)} all-gather(bf16[64,256]{1,0:T(8,128)(2,1)S(1)} %get-tuple-element.317), channel_id=1, replica_groups=mesh['row'=8,'col'=4] {'row'}, dimensions={1}, use_global_device_ids=true | all-gather | bytes 294912 | tf_op jit(solution)/shard_map/while/body/eval_jaxpr/all_gather | solution.py:34
  153.0 0.0 copy-done
  153.0 0.0 copy-done.1
  153.0 0.0 reduce-scatter.3.cloned.1.call-start
  153.0 8.7 %fusion.90 = f32[64,4,1024]{2,0,1:T(8,128)S(1)} fusion(bf16[2,4,1024,2048]{3,2,1,0:T(8,128)(2,1)} %get-tuple-element.325, bf16[64,2048]{1,0:T(8,128)(2,1)S(1)} %get-tuple-element.304), kind=kOutput, calls=%fused_computation.4.clone.1 | convolution fusion | flops 1073741824 | bytes 18087936 | tf_op jit(solution)/shard_map/while/body/eval_jaxpr/dot_general | solution.py:25
  161.7 11.9 %fusion.91 = bf16[64,4,1024]{2,0,1:T(8,128)(2,1)} fusion(f32[64,4,1024]{2,0,1:T(8,128)S(1)} %fusion.90, bf16[2,4,1024,2048]{3,2,1,0:T(8,128)(2,1)} %get-tuple-element.324, bf16[2,64,2048]{2,1,0:T(8,128)(2,1)} %get-tuple-element.323, s32[]{:T(128)S(6)} %copy.18), kind=kOutput, calls=%fused_computation.15.clone.1 | convolution fusion | flops 1074266112 | bytes 18612228 | tf_op jit(solution)/shard_map/while/body/eval_jaxpr/dot_general | solution.py:25
  173.6 0.0 reduce-scatter.3.cloned.1.call-update
  173.6 0.0 reduce-scatter.5.cloned.1.call-start
  173.7 8.7 %fusion.93 = f32[64,4,1024]{2,0,1:T(8,128)S(1)} fusion(bf16[2,4,1024,2048]{3,2,1,0:T(8,128)(2,1)} %get-tuple-element.325, bf16[64,2048]{1,0:T(8,128)(2,1)S(1)} %get-tuple-element.305), kind=kOutput, calls=%fused_computation.clone.1 | convolution fusion | flops 1073741824 | bytes 18087936 | tf_op jit(solution)/shard_map/while/body/eval_jaxpr/dot_general | solution.py:25
  182.4 16.5 %reduce-scatter.3.cloned.1.call-done = bf16[64,4,256]{2,0,1:T(8,128)(2,1)} async-done(((bf16[64,4,1024]{2,0,1:T(8,128)(2,1)}), bf16[64,4,256]{2,0,1:T(8,128)(2,1)}) %reduce-scatter.3.cloned.1.call-update) | async-done | bytes 131088 | tf_op jit(solution)/shard_map/while/body/eval_jaxpr/reduce_scatter | solution.py:41
  198.9 0.9 convert_add_fusion.4
  199.8 0.1 fusion.92
  199.9 0.0 copy-start
  199.9 14.3 %all_gather.20 = bf16[64,2048]{1,0:T(8,128)(2,1)S(1)} all-gather(bf16[64,256]{1,0:T(8,128)(2,1)S(1)} %get-tuple-element.316), channel_id=1, replica_groups=mesh['row'=8,'col'=4] {'row'}, dimensions={1}, use_global_device_ids=true | all-gather | bytes 294912 | tf_op jit(solution)/shard_map/while/body/eval_jaxpr/all_gather | solution.py:34
  214.2 9.7 %fusion.94 = bf16[64,4,1024]{2,0,1:T(8,128)(2,1)} fusion(f32[64,4,1024]{2,0,1:T(8,128)S(1)} %fusion.93, bf16[2,4,1024,2048]{3,2,1,0:T(8,128)(2,1)} %get-tuple-element.324, bf16[64,2048]{1,0:T(8,128)(2,1)S(1)} %all_gather.20), kind=kOutput, calls=%fused_computation.14.clone.1 | convolution fusion | flops 1074266112 | bytes 18612224 | tf_op jit(solution)/shard_map/while/body/eval_jaxpr/dot_general | solution.py:25
  223.8 0.0 reduce-scatter.5.cloned.1.call-update
  223.9 25.3 %reduce-scatter.5.cloned.1.call-done = bf16[64,4,256]{2,0,1:T(8,128)(2,1)} async-done(((bf16[64,4,1024]{2,0,1:T(8,128)(2,1)}), bf16[64,4,256]{2,0,1:T(8,128)(2,1)}) %reduce-scatter.5.cloned.1.call-update) | async-done | bytes 131088 | tf_op jit(solution)/shard_map/while/body/eval_jaxpr/reduce_scatter | solution.py:41
  249.1 0.9 convert_add_fusion.5
  250.1 0.1 bitcast_dynamic-update-slice_fusion.2
  250.2 0.0 copy-start.1
  250.2 14.3 %all_gather.21 = bf16[64,2048]{1,0:T(8,128)(2,1)S(1)} all-gather(bf16[64,256]{1,0:T(8,128)(2,1)S(1)} %get-tuple-element.317), channel_id=1, replica_groups=mesh['row'=8,'col'=4] {'row'}, dimensions={1}, use_global_device_ids=true | all-gather | bytes 294912 | tf_op jit(solution)/shard_map/while/body/eval_jaxpr/all_gather | solution.py:34
  264.5 0.0 copy-done
  264.5 0.0 copy-done.1
  264.5 0.0 copy-start.2
  264.5 0.7 pad_maximum_fusion
  265.2 1.4 pad_maximum_fusion.1
  266.6 0.0 copy-done.2
  (2 shorter events, 0.0 us)
Async XLA Ops:
  40.3 47.1 %reduce-scatter.3.cloned.1.call-start = ((), (), s32[]{:S(2)}) async-start(), calls=%async_computation.2 | async-start | bytes 655360 | tf_op jit(solution)/shard_map/while/body/eval_jaxpr/reduce_scatter | solution.py:41
  61.0 76.6 %reduce-scatter.5.cloned.1.call-start = ((), (), s32[]{:S(2)}) async-start(), calls=%async_computation.3 | async-start | bytes 655360 | tf_op jit(solution)/shard_map/while/body/eval_jaxpr/reduce_scatter | solution.py:41
  88.4 64.6 %copy-start = (bf16[64,256]{1,0:T(8,128)(2,1)}, bf16[64,256]{1,0:T(8,128)(2,1)S(1)}, u32[]{:S(2)}) copy-start(bf16[64,256]{1,0:T(8,128)(2,1)S(1)} %get-tuple-element.316) | copy-start | bytes 98308 | tf_op jit(solution)/shard_map/while
  138.6 14.3 %copy-start.1 = (bf16[64,256]{1,0:T(8,128)(2,1)}, bf16[64,256]{1,0:T(8,128)(2,1)S(1)}, u32[]{:S(2)}) copy-start(bf16[64,256]{1,0:T(8,128)(2,1)S(1)} %get-tuple-element.317) | copy-start | bytes 98308 | tf_op jit(solution)/shard_map/while
  153.0 45.9 %reduce-scatter.3.cloned.1.call-start = ((), (), s32[]{:S(2)}) async-start(), calls=%async_computation.2 | async-start | bytes 655360 | tf_op jit(solution)/shard_map/while/body/eval_jaxpr/reduce_scatter | solution.py:41
  173.6 75.5 %reduce-scatter.5.cloned.1.call-start = ((), (), s32[]{:S(2)}) async-start(), calls=%async_computation.3 | async-start | bytes 655360 | tf_op jit(solution)/shard_map/while/body/eval_jaxpr/reduce_scatter | solution.py:41
  199.9 64.6 %copy-start = (bf16[64,256]{1,0:T(8,128)(2,1)}, bf16[64,256]{1,0:T(8,128)(2,1)S(1)}, u32[]{:S(2)}) copy-start(bf16[64,256]{1,0:T(8,128)(2,1)S(1)} %get-tuple-element.316) | copy-start | bytes 98308 | tf_op jit(solution)/shard_map/while
  250.2 14.3 %copy-start.1 = (bf16[64,256]{1,0:T(8,128)(2,1)}, bf16[64,256]{1,0:T(8,128)(2,1)S(1)}, u32[]{:S(2)}) copy-start(bf16[64,256]{1,0:T(8,128)(2,1)S(1)} %get-tuple-element.317) | copy-start | bytes 98308 | tf_op jit(solution)/shard_map/while
  264.5 2.1 copy-start.2
Sparse Core Ops, SparseCore 0:
  61.1 26.2 reduce-scatter.2
  112.6 25.0 reduce-scatter.4
  173.7 25.0 reduce-scatter.2
  224.0 25.1 reduce-scatter.4
where the time goes:
time: 274 us; the launch traced here: 273 us
  blocking collectives  87.3 us (32%)
  waiting for transfers between devices  84.6 us (31%)
  matrix products  78.1 us (29%)
  between operations  13.7 us (5%)
  other arithmetic  6.13 us (2%)
  local copies, waits for them, and re-layouts  3.06 us (1%)
    all_gather x6, blocking collectives, to_columns(): return lax.all_gather(owned, 'row', axis=1, tiled=True)  87.3 us
    reduce_scatter x4, waiting for transfers between devices, gate_sums(): lax.psum_scatter(partial_value.astype(jnp.bfloat16), 'col', scatter_dimen...  84.5 us
    dot_general x8, matrix products, project(): lax.dot_general(flattened, weight.reshape(-1, weight.shape[-1]), (((1,),...  78.1 us
  transfers between devices with their start and end apart: 4, of which 4 were waited for; matrix products, arithmetic and copies ran while one was open for 6% of the time, Pallas kernels for 0%

commit v1 on v0

--- a/solution.py
+++ b/solution.py
@@ -2,6 +2,19 @@
 import jax.numpy as jnp
 from jax import lax
 from jax.sharding import PartitionSpec as P
+
+
+def collect(x, axis, dim):
+    ways = lax.axis_size(axis)
+    up = [(d, (d + 1) % ways) for d in range(ways)]
+    down = [(d, (d - 1) % ways) for d in range(ways)]
+    earlier, later = ([x], [x])
+    for _ in range(ways // 2):
+        earlier.append(lax.ppermute(earlier[-1], axis, up))
+    for _ in range((ways - 1) // 2):
+        later.append(lax.ppermute(later[-1], axis, down))
+    line = jnp.concatenate([*earlier[::-1], *later[1:]], axis=dim)
+    return jnp.roll(line, (lax.axis_index(axis) - ways // 2) * x.shape[dim], axis=dim)
 
 
 def lstm_cell(gate_total, cell_state):
@@ -31,7 +44,7 @@
         return result.reshape(leading + (4, block_rows))
 
     def to_columns(owned):
-        return lax.all_gather(owned, "row", axis=1, tiled=True)
+        return collect(owned, "row", 1)
 
     def gate_sums(partial_value, layer):
         bias_part = lax.dynamic_slice_in_dim(

time: 274 us -> 313 us (1.14)
  blocking collectives: 87.3 us -> 0 us
  waiting for transfers between devices: 84.6 us -> 152 us
  starting transfers between devices: 0.13 us -> 57.2 us
    all_gather x6 -> x0, blocking collectives: 87.3 us -> none  [to_columns(): return lax.all_gather(owned, 'row', axis=1, tiled=True)]
    ppermute x0 -> x42, starting transfers between devices: none -> 57.1 us  [the longest x18 52.7 us: collect(): later.append(lax.ppermute(later[-1], axis, down))]
    ppermute x0 -> x42, waiting for transfers between devices: none -> 52 us  [the longest x24 48.3 us: collect(): earlier.append(lax.ppermute(earlier[-1], axis, up))]
    reduce_scatter x4, waiting for transfers between devices: 84.5 us -> 100 us  [gate_sums(): lax.psum_scatter(partial_value.astype(jnp.bfloat16), 'col', scatter_dimen...]
  transfers between devices with their start and end apart: 4 -> 46, of which waited for: 4 -> 26; matrix products, arithmetic and copies ran while one was open for 6% -> 6% of each run, Pallas kernels for 0% -> 0%
where the time goes in v1:
time: 313 us; the launch traced here: 312 us
  waiting for transfers between devices  152 us (49%)
  matrix products  78 us (25%)
  starting transfers between devices  57.2 us (18%)
  between operations  13.9 us (4%)
  other arithmetic  7.04 us (2%)
  local copies, waits for them, and re-layouts  3.41 us (1%)
    reduce_scatter x4, waiting for transfers between devices, gate_sums(): lax.psum_scatter(partial_value.astype(jnp.bfloat16), 'col', scatter_dimen...  100 us
    dot_general x8, matrix products, project(): lax.dot_general(flattened, weight.reshape(-1, weight.shape[-1]), (((1,),...  78 us
    ppermute x18, starting transfers between devices, collect(): later.append(lax.ppermute(later[-1], axis, down))  52.7 us
    ppermute x24, waiting for transfers between devices, collect(): earlier.append(lax.ppermute(earlier[-1], axis, up))  48.3 us
  transfers between devices with their start and end apart: 46, of which 26 were waited for; matrix products, arithmetic and copies ran while one was open for 6% of the time, Pallas kernels for 0%

profile of v1, /device:TPU:0, one launch (start us, length us, event | category | flops | bytes accessed | tf_op | source)
XLA Modules:
  0.0 312.4 jit_solution(4672948864040450634)
XLA Ops:
  7.2 0.8 slice_bitcast_fusion.2
  8.0 0.5 collective-permute-start.14
  8.5 2.7 collective-permute-start.21
  11.2 1.5 collective-permute-start.25
  12.7 0.7 collective-permute-start.18
  13.3 0.8 collective-permute-done.14
  14.1 0.9 slice_bitcast_fusion
  15.5 3.8 %collective-permute-done.15 = bf16[64,256]{1,0:T(8,128)(2,1)S(1)} collective-permute-done((bf16[64,256]{1,0:T(8,128)(2,1)S(1)}, bf16[64,256]{1,0:T(8,128)(2,1)S(1)}, u32[]{:S(2)}, u32[]{:S(2)}) %collective-permute-start.15) | collective-permute-done | bytes 32800 | tf_op jit(solution)/shard_map/ppermute | solution.py:13
  19.3 0.7 fusion.71
  20.0 3.5 %collective-permute-start.26 = (bf16[64,256]{1,0:T(8,128)(2,1)S(1)}, bf16[64,256]{1,0:T(8,128)(2,1)S(1)}, u32[]{:S(2)}, u32[]{:S(2)}) collective-permute-start(bf16[64,256]{1,0:T(8,128)(2,1)S(1)} %collective-permute-done.25), channel_id=1, source_target_pairs={{0,28},{4,0},{8,4},{12,8},{16,12},{20,16},{24,20},{28,24},{1,29},{... | collective-permute-start | bytes 98312 | tf_op jit(solution)/shard_map/ppermute | solution.py:15
  24.1 0.7 collective-permute-done.16
  24.8 0.6 collective-permute-done.26
  25.3 3.7 %collective-permute-start.27 = (bf16[64,256]{1,0:T(8,128)(2,1)S(1)}, bf16[64,256]{1,0:T(8,128)(2,1)S(1)}, u32[]{:S(2)}, u32[]{:S(2)}) collective-permute-start(bf16[64,256]{1,0:T(8,128)(2,1)S(1)} %collective-permute-done.26), channel_id=1, source_target_pairs={{0,28},{4,0},{8,4},{12,8},{16,12},{20,16},{24,20},{28,24},{1,29},{... | collective-permute-start | bytes 98312 | tf_op jit(solution)/shard_map/ppermute | solution.py:15
  29.0 0.6 collective-permute-start.20
  29.7 0.5 collective-permute-done.17
  30.2 4.6 %collective-permute-done.24 = bf16[64,256]{1,0:T(8,128)(2,1)S(1)} collective-permute-done((bf16[64,256]{1,0:T(8,128)(2,1)S(1)}, bf16[64,256]{1,0:T(8,128)(2,1)S(1)}, u32[]{:S(2)}, u32[]{:S(2)}) %collective-permute-start.24) | collective-permute-done | bytes 32800 | tf_op jit(solution)/shard_map/ppermute | solution.py:13
  34.8 0.8 constant_dynamic-update-slice_fusion.27
  36.1 267.7 %while.24 = (s32[]{:T(128)}, bf16[64,256]{1,0:T(8,128)(2,1)}, bf16[64,256]{1,0:T(8,128)(2,1)}, bf16[64,2048]{1,0:T(8,128)(2,1)S(1)}, bf16[64,2048]{1,0:T(8,128)(...) while((s32[]{:T(128)}, bf16[64,256]{1,0:T(8,128)(2,1)}, ...), condition=%wide.region_3.5_spmd, body=%wide.region_0.4_spmd.sunk | while | flops 4297785344 | bytes 83207752 | solution.py:87
  36.1 8.7 %fusion.95 = f32[64,4,1024]{2,0,1:T(8,128)S(1)} fusion(bf16[2,4,1024,2048]{3,2,1,0:T(8,128)(2,1)} %get-tuple-element.354, bf16[64,2048]{1,0:T(8,128)(2,1)S(1)} %get-tuple-element.325), kind=kOutput, calls=%fused_computation.4.clone.1 | convolution fusion | flops 1073741824 | bytes 18087936 | tf_op jit(solution)/shard_map/while/body/eval_jaxpr/dot_general | solution.py:38
  44.9 11.9 %fusion.96 = bf16[64,4,1024]{2,0,1:T(8,128)(2,1)} fusion(f32[64,4,1024]{2,0,1:T(8,128)S(1)} %fusion.95, bf16[2,4,1024,2048]{3,2,1,0:T(8,128)(2,1)} %get-tuple-element.353, bf16[2,64,2048]{2,1,0:T(8,128)(2,1)} %get-tuple-element.352, s32[]{:T(128)} %get-tuple-element.322), kind=kOutput, calls=%fused_computation.15.clone.1 | convolution fusion | flops 1074266112 | bytes 18612736 | tf_op jit(solution)/shard_map/while/body/eval_jaxpr/dot_general | solution.py:38
  56.8 24.0 %reduce-scatter.3.cloned.1.call-done = bf16[64,4,256]{2,0,1:T(8,128)(2,1)} async-done(((bf16[64,4,1024]{2,0,1:T(8,128)(2,1)}), bf16[64,4,256]{2,0,1:T(8,128)(2,1)}) %reduce-scatter.3.cloned.1.call-update) | async-done | bytes 131088 | tf_op jit(solution)/shard_map/while/body/eval_jaxpr/reduce_scatter | solution.py:54
  80.8 0.9 convert_add_fusion.4
  81.9 5.1 %collective-permute-done = bf16[64,256]{1,0:T(8,128)(2,1)S(1)} collective-permute-done((bf16[64,256]{1,0:T(8,128)(2,1)S(1)}, bf16[64,256]{1,0:T(8,128)(2,1)S(1)}, u32[]{:S(2)}, u32[]{:S(2)}) %collective-permute-start) | collective-permute-done | bytes 32800 | tf_op jit(solution)/shard_map/while/body/eval_jaxpr/ppermute | solution.py:13
  87.0 3.5 %collective-permute-start.4 = (bf16[64,256]{1,0:T(8,128)(2,1)S(1)}, bf16[64,256]{1,0:T(8,128)(2,1)S(1)}, u32[]{:S(2)}, u32[]{:S(2)}) collective-permute-start(bf16[64,256]{1,0:T(8,128)(2,1)S(1)} %get-tuple-element.345), channel_id=1, source_target_pairs={{0,28},{4,0},{8,4},{12,8},{16,12},{20,16},{24,20},{28,24},{1,29},{... | collective-permute-start | bytes 98312 | tf_op jit(solution)/shard_map/while/body/eval_jaxpr/ppermute | solution.py:15
  90.5 1.9 collective-permute-done.1
  92.5 3.5 %collective-permute-start.5 = (bf16[64,256]{1,0:T(8,128)(2,1)S(1)}, bf16[64,256]{1,0:T(8,128)(2,1)S(1)}, u32[]{:S(2)}, u32[]{:S(2)}) collective-permute-start(bf16[64,256]{1,0:T(8,128)(2,1)S(1)} %collective-permute-done.4), channel_id=1, source_target_pairs={{0,28},{4,0},{8,4},{12,8},{16,12},{20,16},{24,20},{28,24},{1,29},{... | collective-permute-start | bytes 98312 | tf_op jit(solution)/shard_map/while/body/eval_jaxpr/ppermute | solution.py:15
  96.0 1.6 collective-permute-done.2
  97.6 8.7 %fusion.98 = f32[64,4,1024]{2,0,1:T(8,128)S(1)} fusion(bf16[2,4,1024,2048]{3,2,1,0:T(8,128)(2,1)} %get-tuple-element.354, bf16[64,2048]{1,0:T(8,128)(2,1)S(1)} %get-tuple-element.326), kind=kOutput, calls=%fused_computation.clone.1 | convolution fusion | flops 1073741824 | bytes 18087936 | tf_op jit(solution)/shard_map/while/body/eval_jaxpr/dot_general | solution.py:38
  106.4 3.6 %collective-permute-start.6 = (bf16[64,256]{1,0:T(8,128)(2,1)S(1)}, bf16[64,256]{1,0:T(8,128)(2,1)S(1)}, u32[]{:S(2)}, u32[]{:S(2)}) collective-permute-start(bf16[64,256]{1,0:T(8,128)(2,1)S(1)} %collective-permute-done.5), channel_id=1, source_target_pairs={{0,28},{4,0},{8,4},{12,8},{16,12},{20,16},{24,20},{28,24},{1,29},{... | collective-permute-start | bytes 98312 | tf_op jit(solution)/shard_map/while/body/eval_jaxpr/ppermute | solution.py:15
  110.1 1.5 collective-permute-done.6
  111.7 9.7 %fusion.100 = bf16[64,4,1024]{2,0,1:T(8,128)(2,1)} fusion(f32[64,4,1024]{2,0,1:T(8,128)S(1)} %fusion.98, bf16[2,4,1024,2048]{3,2,1,0:T(8,128)(2,1)} %get-tuple-element.353, bf16[64,2048]{1,0:T(8,128)(2,1)S(1)} %fusion.99), kind=kOutput, calls=%fused_computation.14.clone.1 | convolution fusion | flops 1074266112 | bytes 18612224 | tf_op jit(solution)/shard_map/while/body/eval_jaxpr/dot_general | solution.py:38
  121.4 25.5 %reduce-scatter.5.cloned.1.call-done = bf16[64,4,256]{2,0,1:T(8,128)(2,1)} async-done(((bf16[64,4,1024]{2,0,1:T(8,128)(2,1)}), bf16[64,4,256]{2,0,1:T(8,128)(2,1)}) %reduce-scatter.5.cloned.1.call-update) | async-done | bytes 131088 | tf_op jit(solution)/shard_map/while/body/eval_jaxpr/reduce_scatter | solution.py:54
  146.9 0.9 convert_add_fusion.5
  148.0 5.1 %collective-permute-done.7 = bf16[64,256]{1,0:T(8,128)(2,1)S(1)} collective-permute-done((bf16[64,256]{1,0:T(8,128)(2,1)S(1)}, bf16[64,256]{1,0:T(8,128)(2,1)S(1)}, u32[]{:S(2)}, u32[]{:S(2)}) %collective-permute-start.7) | collective-permute-done | bytes 32800 | tf_op jit(solution)/shard_map/while/body/eval_jaxpr/ppermute | solution.py:13
  153.1 3.5 %collective-permute-start.11 = (bf16[64,256]{1,0:T(8,128)(2,1)S(1)}, bf16[64,256]{1,0:T(8,128)(2,1)S(1)}, u32[]{:S(2)}, u32[]{:S(2)}) collective-permute-start(bf16[64,256]{1,0:T(8,128)(2,1)S(1)} %get-tuple-element.346), channel_id=1, source_target_pairs={{0,28},{4,0},{8,4},{12,8},{16,12},{20,16},{24,20},{28,24},{1,29},{... | collective-permute-start | bytes 98312 | tf_op jit(solution)/shard_map/while/body/eval_jaxpr/ppermute | solution.py:15
  156.7 1.9 collective-permute-done.8
  158.6 3.5 %collective-permute-start.12 = (bf16[64,256]{1,0:T(8,128)(2,1)S(1)}, bf16[64,256]{1,0:T(8,128)(2,1)S(1)}, u32[]{:S(2)}, u32[]{:S(2)}) collective-permute-start(bf16[64,256]{1,0:T(8,128)(2,1)S(1)} %collective-permute-done.11), channel_id=1, source_target_pairs={{0,28},{4,0},{8,4},{12,8},{16,12},{20,16},{24,20},{28,24},{1,29},{... | collective-permute-start | bytes 98312 | tf_op jit(solution)/shard_map/while/body/eval_jaxpr/ppermute | solution.py:15
  162.2 1.7 collective-permute-done.9
  163.9 3.5 %collective-permute-start.13 = (bf16[64,256]{1,0:T(8,128)(2,1)S(1)}, bf16[64,256]{1,0:T(8,128)(2,1)S(1)}, u32[]{:S(2)}, u32[]{:S(2)}) collective-permute-start(bf16[64,256]{1,0:T(8,128)(2,1)S(1)} %collective-permute-done.12), channel_id=1, source_target_pairs={{0,28},{4,0},{8,4},{12,8},{16,12},{20,16},{24,20},{28,24},{1,29},{... | collective-permute-start | bytes 98312 | tf_op jit(solution)/shard_map/while/body/eval_jaxpr/ppermute | solution.py:15
  167.4 1.6 collective-permute-done.10
  169.3 8.7 %fusion.95 = f32[64,4,1024]{2,0,1:T(8,128)S(1)} fusion(bf16[2,4,1024,2048]{3,2,1,0:T(8,128)(2,1)} %get-tuple-element.354, bf16[64,2048]{1,0:T(8,128)(2,1)S(1)} %get-tuple-element.325), kind=kOutput, calls=%fused_computation.4.clone.1 | convolution fusion | flops 1073741824 | bytes 18087936 | tf_op jit(solution)/shard_map/while/body/eval_jaxpr/dot_general | solution.py:38
  178.1 11.9 %fusion.96 = bf16[64,4,1024]{2,0,1:T(8,128)(2,1)} fusion(f32[64,4,1024]{2,0,1:T(8,128)S(1)} %fusion.95, bf16[2,4,1024,2048]{3,2,1,0:T(8,128)(2,1)} %get-tuple-element.353, bf16[2,64,2048]{2,1,0:T(8,128)(2,1)} %get-tuple-element.352, s32[]{:T(128)} %get-tuple-element.322), kind=kOutput, calls=%fused_computation.15.clone.1 | convolution fusion | flops 1074266112 | bytes 18612736 | tf_op jit(solution)/shard_map/while/body/eval_jaxpr/dot_general | solution.py:38
  190.0 25.3 %reduce-scatter.3.cloned.1.call-done = bf16[64,4,256]{2,0,1:T(8,128)(2,1)} async-done(((bf16[64,4,1024]{2,0,1:T(8,128)(2,1)}), bf16[64,4,256]{2,0,1:T(8,128)(2,1)}) %reduce-scatter.3.cloned.1.call-update) | async-done | bytes 131088 | tf_op jit(solution)/shard_map/while/body/eval_jaxpr/reduce_scatter | solution.py:54
  215.3 0.9 convert_add_fusion.4
  216.4 5.1 %collective-permute-done = bf16[64,256]{1,0:T(8,128)(2,1)S(1)} collective-permute-done((bf16[64,256]{1,0:T(8,128)(2,1)S(1)}, bf16[64,256]{1,0:T(8,128)(2,1)S(1)}, u32[]{:S(2)}, u32[]{:S(2)}) %collective-permute-start) | collective-permute-done | bytes 32800 | tf_op jit(solution)/shard_map/while/body/eval_jaxpr/ppermute | solution.py:13
  221.5 3.5 %collective-permute-start.4 = (bf16[64,256]{1,0:T(8,128)(2,1)S(1)}, bf16[64,256]{1,0:T(8,128)(2,1)S(1)}, u32[]{:S(2)}, u32[]{:S(2)}) collective-permute-start(bf16[64,256]{1,0:T(8,128)(2,1)S(1)} %get-tuple-element.345), channel_id=1, source_target_pairs={{0,28},{4,0},{8,4},{12,8},{16,12},{20,16},{24,20},{28,24},{1,29},{... | collective-permute-start | bytes 98312 | tf_op jit(solution)/shard_map/while/body/eval_jaxpr/ppermute | solution.py:15
  225.1 1.9 collective-permute-done.1
  227.0 3.5 %collective-permute-start.5 = (bf16[64,256]{1,0:T(8,128)(2,1)S(1)}, bf16[64,256]{1,0:T(8,128)(2,1)S(1)}, u32[]{:S(2)}, u32[]{:S(2)}) collective-permute-start(bf16[64,256]{1,0:T(8,128)(2,1)S(1)} %collective-permute-done.4), channel_id=1, source_target_pairs={{0,28},{4,0},{8,4},{12,8},{16,12},{20,16},{24,20},{28,24},{1,29},{... | collective-permute-start | bytes 98312 | tf_op jit(solution)/shard_map/while/body/eval_jaxpr/ppermute | solution.py:15
  230.5 1.6 collective-permute-done.2
  232.1 8.7 %fusion.98 = f32[64,4,1024]{2,0,1:T(8,128)S(1)} fusion(bf16[2,4,1024,2048]{3,2,1,0:T(8,128)(2,1)} %get-tuple-element.354, bf16[64,2048]{1,0:T(8,128)(2,1)S(1)} %get-tuple-element.326), kind=kOutput, calls=%fused_computation.clone.1 | convolution fusion | flops 1073741824 | bytes 18087936 | tf_op jit(solution)/shard_map/while/body/eval_jaxpr/dot_general | solution.py:38
  240.9 3.6 %collective-permute-start.6 = (bf16[64,256]{1,0:T(8,128)(2,1)S(1)}, bf16[64,256]{1,0:T(8,128)(2,1)S(1)}, u32[]{:S(2)}, u32[]{:S(2)}) collective-permute-start(bf16[64,256]{1,0:T(8,128)(2,1)S(1)} %collective-permute-done.5), channel_id=1, source_target_pairs={{0,28},{4,0},{8,4},{12,8},{16,12},{20,16},{24,20},{28,24},{1,29},{... | collective-permute-start | bytes 98312 | tf_op jit(solution)/shard_map/while/body/eval_jaxpr/ppermute | solution.py:15
  244.6 1.5 collective-permute-done.6
  246.3 9.7 %fusion.100 = bf16[64,4,1024]{2,0,1:T(8,128)(2,1)} fusion(f32[64,4,1024]{2,0,1:T(8,128)S(1)} %fusion.98, bf16[2,4,1024,2048]{3,2,1,0:T(8,128)(2,1)} %get-tuple-element.353, bf16[64,2048]{1,0:T(8,128)(2,1)S(1)} %fusion.99), kind=kOutput, calls=%fused_computation.14.clone.1 | convolution fusion | flops 1074266112 | bytes 18612224 | tf_op jit(solution)/shard_map/while/body/eval_jaxpr/dot_general | solution.py:38
  255.9 25.5 %reduce-scatter.5.cloned.1.call-done = bf16[64,4,256]{2,0,1:T(8,128)(2,1)} async-done(((bf16[64,4,1024]{2,0,1:T(8,128)(2,1)}), bf16[64,4,256]{2,0,1:T(8,128)(2,1)}) %reduce-scatter.5.cloned.1.call-update) | async-done | bytes 131088 | tf_op jit(solution)/shard_map/while/body/eval_jaxpr/reduce_scatter | solution.py:54
  281.5 0.9 convert_add_fusion.5
  282.6 5.1 %collective-permute-done.7 = bf16[64,256]{1,0:T(8,128)(2,1)S(1)} collective-permute-done((bf16[64,256]{1,0:T(8,128)(2,1)S(1)}, bf16[64,256]{1,0:T(8,128)(2,1)S(1)}, u32[]{:S(2)}, u32[]{:S(2)}) %collective-permute-start.7) | collective-permute-done | bytes 32800 | tf_op jit(solution)/shard_map/while/body/eval_jaxpr/ppermute | solution.py:13
  287.7 3.5 %collective-permute-start.11 = (bf16[64,256]{1,0:T(8,128)(2,1)S(1)}, bf16[64,256]{1,0:T(8,128)(2,1)S(1)}, u32[]{:S(2)}, u32[]{:S(2)}) collective-permute-start(bf16[64,256]{1,0:T(8,128)(2,1)S(1)} %get-tuple-element.346), channel_id=1, source_target_pairs={{0,28},{4,0},{8,4},{12,8},{16,12},{20,16},{24,20},{28,24},{1,29},{... | collective-permute-start | bytes 98312 | tf_op jit(solution)/shard_map/while/body/eval_jaxpr/ppermute | solution.py:15
  291.2 1.9 collective-permute-done.8
  293.1 3.5 %collective-permute-start.12 = (bf16[64,256]{1,0:T(8,128)(2,1)S(1)}, bf16[64,256]{1,0:T(8,128)(2,1)S(1)}, u32[]{:S(2)}, u32[]{:S(2)}) collective-permute-start(bf16[64,256]{1,0:T(8,128)(2,1)S(1)} %collective-permute-done.11), channel_id=1, source_target_pairs={{0,28},{4,0},{8,4},{12,8},{16,12},{20,16},{24,20},{28,24},{1,29},{... | collective-permute-start | bytes 98312 | tf_op jit(solution)/shard_map/while/body/eval_jaxpr/ppermute | solution.py:15
  296.7 1.7 collective-permute-done.9
  298.4 3.5 %collective-permute-start.13 = (bf16[64,256]{1,0:T(8,128)(2,1)S(1)}, bf16[64,256]{1,0:T(8,128)(2,1)S(1)}, u32[]{:S(2)}, u32[]{:S(2)}) collective-permute-start(bf16[64,256]{1,0:T(8,128)(2,1)S(1)} %collective-permute-done.12), channel_id=1, source_target_pairs={{0,28},{4,0},{8,4},{12,8},{16,12},{20,16},{24,20},{28,24},{1,29},{... | collective-permute-start | bytes 98312 | tf_op jit(solution)/shard_map/while/body/eval_jaxpr/ppermute | solution.py:15
  301.9 1.6 collective-permute-done.10
  303.8 0.7 pad_maximum_fusion
  304.5 1.4 pad_maximum_fusion.1
  (123 shorter events, 3.0 us)
Async XLA Ops:
  7.9 28.1 %copy-start = (bf16[64,256]{1,0:T(8,128)(2,1)}, bf16[64,256]{1,0:T(8,128)(2,1)S(1)}, u32[]{:S(2)}) copy-start(bf16[64,256]{1,0:T(8,128)(2,1)S(1)} %get-tuple-element.302) | copy-start | bytes 98308
  7.9 28.1 %copy-start.2 = (bf16[64,256]{1,0:T(8,128)(2,1)}, bf16[64,256]{1,0:T(8,128)(2,1)S(1)}, u32[]{:S(2)}) copy-start(bf16[64,256]{1,0:T(8,128)(2,1)S(1)} %get-tuple-element.301) | copy-start | bytes 98308
  8.0 6.2 %collective-permute-start.14 = (bf16[64,256]{1,0:T(8,128)(2,1)S(1)}, bf16[64,256]{1,0:T(8,128)(2,1)S(1)}, u32[]{:S(2)}, u32[]{:S(2)}) collective-permute-start(bf16[64,256]{1,0:T(8,128)(2,1)S(1)} %get-tuple-element.301), channel_id=1, source_target_pairs={{0,4},{4,8},{8,12},{12,16},{16,20},{20,24},{24,28},{28,0},{1,5},{5... | collective-permute-start | bytes 98312 | tf_op jit(solution)/shard_map/ppermute | solution.py:13
  8.5 6.5 %collective-permute-start.21 = (bf16[64,256]{1,0:T(8,128)(2,1)S(1)}, bf16[64,256]{1,0:T(8,128)(2,1)S(1)}, u32[]{:S(2)}, u32[]{:S(2)}) collective-permute-start(bf16[64,256]{1,0:T(8,128)(2,1)S(1)} %get-tuple-element.302), channel_id=1, source_target_pairs={{0,4},{4,8},{8,12},{12,16},{16,20},{20,24},{24,28},{28,0},{1,5},{5... | collective-permute-start | bytes 98312 | tf_op jit(solution)/shard_map/ppermute | solution.py:13
  11.2 8.8 %collective-permute-start.25 = (bf16[64,256]{1,0:T(8,128)(2,1)S(1)}, bf16[64,256]{1,0:T(8,128)(2,1)S(1)}, u32[]{:S(2)}, u32[]{:S(2)}) collective-permute-start(bf16[64,256]{1,0:T(8,128)(2,1)S(1)} %get-tuple-element.302), channel_id=1, source_target_pairs={{0,28},{4,0},{8,4},{12,8},{16,12},{20,16},{24,20},{28,24},{1,29},{... | collective-permute-start | bytes 98312 | tf_op jit(solution)/shard_map/ppermute | solution.py:15
  12.7 10.9 %collective-permute-start.18 = (bf16[64,256]{1,0:T(8,128)(2,1)S(1)}, bf16[64,256]{1,0:T(8,128)(2,1)S(1)}, u32[]{:S(2)}, u32[]{:S(2)}) collective-permute-start(bf16[64,256]{1,0:T(8,128)(2,1)S(1)} %get-tuple-element.301), channel_id=1, source_target_pairs={{0,28},{4,0},{8,4},{12,8},{16,12},{20,16},{24,20},{28,24},{1,29},{... | collective-permute-start | bytes 98312 | tf_op jit(solution)/shard_map/ppermute | solution.py:15
  14.1 5.1 %collective-permute-start.15 = (bf16[64,256]{1,0:T(8,128)(2,1)S(1)}, bf16[64,256]{1,0:T(8,128)(2,1)S(1)}, u32[]{:S(2)}, u32[]{:S(2)}) collective-permute-start(bf16[64,256]{1,0:T(8,128)(2,1)S(1)} %collective-permute-done.14), channel_id=1, source_target_pairs={{0,4},{4,8},{8,12},{12,16},{16,20},{20,24},{24,28},{28,0},{1,5},{5... | collective-permute-start | bytes 98312 | tf_op jit(solution)/shard_map/ppermute | solution.py:13
  15.0 8.6 %collective-permute-start.22 = (bf16[64,256]{1,0:T(8,128)(2,1)S(1)}, bf16[64,256]{1,0:T(8,128)(2,1)S(1)}, u32[]{:S(2)}, u32[]{:S(2)}) collective-permute-start(bf16[64,256]{1,0:T(8,128)(2,1)S(1)} %collective-permute-done.21), channel_id=1, source_target_pairs={{0,4},{4,8},{8,12},{12,16},{16,20},{20,24},{24,28},{28,0},{1,5},{5... | collective-permute-start | bytes 98312 | tf_op jit(solution)/shard_map/ppermute | solution.py:13
  19.3 5.5 %collective-permute-start.16 = (bf16[64,256]{1,0:T(8,128)(2,1)S(1)}, bf16[64,256]{1,0:T(8,128)(2,1)S(1)}, u32[]{:S(2)}, u32[]{:S(2)}) collective-permute-start(bf16[64,256]{1,0:T(8,128)(2,1)S(1)} %collective-permute-done.15), channel_id=1, source_target_pairs={{0,4},{4,8},{8,12},{12,16},{16,20},{20,24},{24,28},{28,0},{1,5},{5... | collective-permute-start | bytes 98312 | tf_op jit(solution)/shard_map/ppermute | solution.py:13
  20.0 5.3 %collective-permute-start.26 = (bf16[64,256]{1,0:T(8,128)(2,1)S(1)}, bf16[64,256]{1,0:T(8,128)(2,1)S(1)}, u32[]{:S(2)}, u32[]{:S(2)}) collective-permute-start(bf16[64,256]{1,0:T(8,128)(2,1)S(1)} %collective-permute-done.25), channel_id=1, source_target_pairs={{0,28},{4,0},{8,4},{12,8},{16,12},{20,16},{24,20},{28,24},{1,29},{... | collective-permute-start | bytes 98312 | tf_op jit(solution)/shard_map/ppermute | solution.py:15
  23.6 5.5 %collective-permute-start.19 = (bf16[64,256]{1,0:T(8,128)(2,1)S(1)}, bf16[64,256]{1,0:T(8,128)(2,1)S(1)}, u32[]{:S(2)}, u32[]{:S(2)}) collective-permute-start(bf16[64,256]{1,0:T(8,128)(2,1)S(1)} %collective-permute-done.18), channel_id=1, source_target_pairs={{0,28},{4,0},{8,4},{12,8},{16,12},{20,16},{24,20},{28,24},{1,29},{... | collective-permute-start | bytes 98312 | tf_op jit(solution)/shard_map/ppermute | solution.py:15
  23.6 6.1 %collective-permute-start.23 = (bf16[64,256]{1,0:T(8,128)(2,1)S(1)}, bf16[64,256]{1,0:T(8,128)(2,1)S(1)}, u32[]{:S(2)}, u32[]{:S(2)}) collective-permute-start(bf16[64,256]{1,0:T(8,128)(2,1)S(1)} %collective-permute-done.22), channel_id=1, source_target_pairs={{0,4},{4,8},{8,12},{12,16},{16,20},{20,24},{24,28},{28,0},{1,5},{5... | collective-permute-start | bytes 98312 | tf_op jit(solution)/shard_map/ppermute | solution.py:13
  24.8 5.4 %collective-permute-start.17 = (bf16[64,256]{1,0:T(8,128)(2,1)S(1)}, bf16[64,256]{1,0:T(8,128)(2,1)S(1)}, u32[]{:S(2)}, u32[]{:S(2)}) collective-permute-start(bf16[64,256]{1,0:T(8,128)(2,1)S(1)} %collective-permute-done.16), channel_id=1, source_target_pairs={{0,4},{4,8},{8,12},{12,16},{16,20},{20,24},{24,28},{28,0},{1,5},{5... | collective-permute-start | bytes 98312 | tf_op jit(solution)/shard_map/ppermute | solution.py:13
  25.3 10.3 %collective-permute-start.27 = (bf16[64,256]{1,0:T(8,128)(2,1)S(1)}, bf16[64,256]{1,0:T(8,128)(2,1)S(1)}, u32[]{:S(2)}, u32[]{:S(2)}) collective-permute-start(bf16[64,256]{1,0:T(8,128)(2,1)S(1)} %collective-permute-done.26), channel_id=1, source_target_pairs={{0,28},{4,0},{8,4},{12,8},{16,12},{20,16},{24,20},{28,24},{1,29},{... | collective-permute-start | bytes 98312 | tf_op jit(solution)/shard_map/ppermute | solution.py:15
  29.0 6.8 %collective-permute-start.20 = (bf16[64,256]{1,0:T(8,128)(2,1)S(1)}, bf16[64,256]{1,0:T(8,128)(2,1)S(1)}, u32[]{:S(2)}, u32[]{:S(2)}) collective-permute-start(bf16[64,256]{1,0:T(8,128)(2,1)S(1)} %collective-permute-done.19), channel_id=1, source_target_pairs={{0,28},{4,0},{8,4},{12,8},{16,12},{20,16},{24,20},{28,24},{1,29},{... | collective-permute-start | bytes 98312 | tf_op jit(solution)/shard_map/ppermute | solution.py:15
  29.7 5.1 %collective-permute-start.24 = (bf16[64,256]{1,0:T(8,128)(2,1)S(1)}, bf16[64,256]{1,0:T(8,128)(2,1)S(1)}, u32[]{:S(2)}, u32[]{:S(2)}) collective-permute-start(bf16[64,256]{1,0:T(8,128)(2,1)S(1)} %collective-permute-done.23), channel_id=1, source_target_pairs={{0,4},{4,8},{8,12},{12,16},{16,20},{20,24},{24,28},{28,0},{1,5},{5... | collective-permute-start | bytes 98312 | tf_op jit(solution)/shard_map/ppermute | solution.py:13
  36.1 44.7 %reduce-scatter.3.cloned.1.call-start = ((), (), s32[]{:S(2)}) async-start(), calls=%async_computation.2 | async-start | bytes 655360 | tf_op jit(solution)/shard_map/while/body/eval_jaxpr/reduce_scatter | solution.py:54
  56.8 90.1 %reduce-scatter.5.cloned.1.call-start = ((), (), s32[]{:S(2)}) async-start(), calls=%async_computation.3 | async-start | bytes 655360 | tf_op jit(solution)/shard_map/while/body/eval_jaxpr/reduce_scatter | solution.py:54
  81.8 87.4 %copy-start.3 = (bf16[64,256]{1,0:T(8,128)(2,1)}, bf16[64,256]{1,0:T(8,128)(2,1)S(1)}, u32[]{:S(2)}) copy-start(bf16[64,256]{1,0:T(8,128)(2,1)S(1)} %get-tuple-element.345) | copy-start | bytes 98308 | tf_op jit(solution)/shard_map/while
  81.8 5.2 %collective-permute-start = (bf16[64,256]{1,0:T(8,128)(2,1)S(1)}, bf16[64,256]{1,0:T(8,128)(2,1)S(1)}, u32[]{:S(2)}, u32[]{:S(2)}) collective-permute-start(bf16[64,256]{1,0:T(8,128)(2,1)S(1)} %get-tuple-element.345), channel_id=1, source_target_pairs={{0,4},{4,8},{8,12},{12,16},{16,20},{20,24},{24,28},{28,0},{1,5},{5... | collective-permute-start | bytes 98312 | tf_op jit(solution)/shard_map/while/body/eval_jaxpr/ppermute | solution.py:13
  87.0 5.5 %collective-permute-start.1 = (bf16[64,256]{1,0:T(8,128)(2,1)S(1)}, bf16[64,256]{1,0:T(8,128)(2,1)S(1)}, u32[]{:S(2)}, u32[]{:S(2)}) collective-permute-start(bf16[64,256]{1,0:T(8,128)(2,1)S(1)} %collective-permute-done), channel_id=1, source_target_pairs={{0,4},{4,8},{8,12},{12,16},{16,20},{20,24},{24,28},{28,0},{1,5},{5... | collective-permute-start | bytes 98312 | tf_op jit(solution)/shard_map/while/body/eval_jaxpr/ppermute | solution.py:13
  87.0 5.5 %collective-permute-start.4 = (bf16[64,256]{1,0:T(8,128)(2,1)S(1)}, bf16[64,256]{1,0:T(8,128)(2,1)S(1)}, u32[]{:S(2)}, u32[]{:S(2)}) collective-permute-start(bf16[64,256]{1,0:T(8,128)(2,1)S(1)} %get-tuple-element.345), channel_id=1, source_target_pairs={{0,28},{4,0},{8,4},{12,8},{16,12},{20,16},{24,20},{28,24},{1,29},{... | collective-permute-start | bytes 98312 | tf_op jit(solution)/shard_map/while/body/eval_jaxpr/ppermute | solution.py:15
  92.5 5.1 %collective-permute-start.2 = (bf16[64,256]{1,0:T(8,128)(2,1)S(1)}, bf16[64,256]{1,0:T(8,128)(2,1)S(1)}, u32[]{:S(2)}, u32[]{:S(2)}) collective-permute-start(bf16[64,256]{1,0:T(8,128)(2,1)S(1)} %collective-permute-done.1), channel_id=1, source_target_pairs={{0,4},{4,8},{8,12},{12,16},{16,20},{20,24},{24,28},{28,0},{1,5},{5... | collective-permute-start | bytes 98312 | tf_op jit(solution)/shard_map/while/body/eval_jaxpr/ppermute | solution.py:13
  92.5 13.9 %collective-permute-start.5 = (bf16[64,256]{1,0:T(8,128)(2,1)S(1)}, bf16[64,256]{1,0:T(8,128)(2,1)S(1)}, u32[]{:S(2)}, u32[]{:S(2)}) collective-permute-start(bf16[64,256]{1,0:T(8,128)(2,1)S(1)} %collective-permute-done.4), channel_id=1, source_target_pairs={{0,28},{4,0},{8,4},{12,8},{16,12},{20,16},{24,20},{28,24},{1,29},{... | collective-permute-start | bytes 98312 | tf_op jit(solution)/shard_map/while/body/eval_jaxpr/ppermute | solution.py:15
  97.6 12.4 %collective-permute-start.3 = (bf16[64,256]{1,0:T(8,128)(2,1)S(1)}, bf16[64,256]{1,0:T(8,128)(2,1)S(1)}, u32[]{:S(2)}, u32[]{:S(2)}) collective-permute-start(bf16[64,256]{1,0:T(8,128)(2,1)S(1)} %collective-permute-done.2), channel_id=1, source_target_pairs={{0,4},{4,8},{8,12},{12,16},{16,20},{20,24},{24,28},{28,0},{1,5},{5... | collective-permute-start | bytes 98312 | tf_op jit(solution)/shard_map/while/body/eval_jaxpr/ppermute | solution.py:13
  106.4 5.2 %collective-permute-start.6 = (bf16[64,256]{1,0:T(8,128)(2,1)S(1)}, bf16[64,256]{1,0:T(8,128)(2,1)S(1)}, u32[]{:S(2)}, u32[]{:S(2)}) collective-permute-start(bf16[64,256]{1,0:T(8,128)(2,1)S(1)} %collective-permute-done.5), channel_id=1, source_target_pairs={{0,28},{4,0},{8,4},{12,8},{16,12},{20,16},{24,20},{28,24},{1,29},{... | collective-permute-start | bytes 98312 | tf_op jit(solution)/shard_map/while/body/eval_jaxpr/ppermute | solution.py:15
  147.9 21.3 %copy-start.1 = (bf16[64,256]{1,0:T(8,128)(2,1)}, bf16[64,256]{1,0:T(8,128)(2,1)S(1)}, u32[]{:S(2)}) copy-start(bf16[64,256]{1,0:T(8,128)(2,1)S(1)} %get-tuple-element.346) | copy-start | bytes 98308 | tf_op jit(solution)/shard_map/while
  147.9 5.2 %collective-permute-start.7 = (bf16[64,256]{1,0:T(8,128)(2,1)S(1)}, bf16[64,256]{1,0:T(8,128)(2,1)S(1)}, u32[]{:S(2)}, u32[]{:S(2)}) collective-permute-start(bf16[64,256]{1,0:T(8,128)(2,1)S(1)} %get-tuple-element.346), channel_id=1, source_target_pairs={{0,4},{4,8},{8,12},{12,16},{16,20},{20,24},{24,28},{28,0},{1,5},{5... | collective-permute-start | bytes 98312 | tf_op jit(solution)/shard_map/while/body/eval_jaxpr/ppermute | solution.py:13
  153.1 5.5 %collective-permute-start.8 = (bf16[64,256]{1,0:T(8,128)(2,1)S(1)}, bf16[64,256]{1,0:T(8,128)(2,1)S(1)}, u32[]{:S(2)}, u32[]{:S(2)}) collective-permute-start(bf16[64,256]{1,0:T(8,128)(2,1)S(1)} %collective-permute-done.7), channel_id=1, source_target_pairs={{0,4},{4,8},{8,12},{12,16},{16,20},{20,24},{24,28},{28,0},{1,5},{5... | collective-permute-start | bytes 98312 | tf_op jit(solution)/shard_map/while/body/eval_jaxpr/ppermute | solution.py:13
  153.1 5.5 %collective-permute-start.11 = (bf16[64,256]{1,0:T(8,128)(2,1)S(1)}, bf16[64,256]{1,0:T(8,128)(2,1)S(1)}, u32[]{:S(2)}, u32[]{:S(2)}) collective-permute-start(bf16[64,256]{1,0:T(8,128)(2,1)S(1)} %get-tuple-element.346), channel_id=1, source_target_pairs={{0,28},{4,0},{8,4},{12,8},{16,12},{20,16},{24,20},{28,24},{1,29},{... | collective-permute-start | bytes 98312 | tf_op jit(solution)/shard_map/while/body/eval_jaxpr/ppermute | solution.py:15
  158.6 5.2 %collective-permute-start.9 = (bf16[64,256]{1,0:T(8,128)(2,1)S(1)}, bf16[64,256]{1,0:T(8,128)(2,1)S(1)}, u32[]{:S(2)}, u32[]{:S(2)}) collective-permute-start(bf16[64,256]{1,0:T(8,128)(2,1)S(1)} %collective-permute-done.8), channel_id=1, source_target_pairs={{0,4},{4,8},{8,12},{12,16},{16,20},{20,24},{24,28},{28,0},{1,5},{5... | collective-permute-start | bytes 98312 | tf_op jit(solution)/shard_map/while/body/eval_jaxpr/ppermute | solution.py:13
  158.6 5.2 %collective-permute-start.12 = (bf16[64,256]{1,0:T(8,128)(2,1)S(1)}, bf16[64,256]{1,0:T(8,128)(2,1)S(1)}, u32[]{:S(2)}, u32[]{:S(2)}) collective-permute-start(bf16[64,256]{1,0:T(8,128)(2,1)S(1)} %collective-permute-done.11), channel_id=1, source_target_pairs={{0,28},{4,0},{8,4},{12,8},{16,12},{20,16},{24,20},{28,24},{1,29},{... | collective-permute-start | bytes 98312 | tf_op jit(solution)/shard_map/while/body/eval_jaxpr/ppermute | solution.py:15
  163.8 5.1 %collective-permute-start.10 = (bf16[64,256]{1,0:T(8,128)(2,1)S(1)}, bf16[64,256]{1,0:T(8,128)(2,1)S(1)}, u32[]{:S(2)}, u32[]{:S(2)}) collective-permute-start(bf16[64,256]{1,0:T(8,128)(2,1)S(1)} %collective-permute-done.9), channel_id=1, source_target_pairs={{0,4},{4,8},{8,12},{12,16},{16,20},{20,24},{24,28},{28,0},{1,5},{5... | collective-permute-start | bytes 98312 | tf_op jit(solution)/shard_map/while/body/eval_jaxpr/ppermute | solution.py:13
  163.9 5.2 %collective-permute-start.13 = (bf16[64,256]{1,0:T(8,128)(2,1)S(1)}, bf16[64,256]{1,0:T(8,128)(2,1)S(1)}, u32[]{:S(2)}, u32[]{:S(2)}) collective-permute-start(bf16[64,256]{1,0:T(8,128)(2,1)S(1)} %collective-permute-done.12), channel_id=1, source_target_pairs={{0,28},{4,0},{8,4},{12,8},{16,12},{20,16},{24,20},{28,24},{1,29},{... | collective-permute-start | bytes 98312 | tf_op jit(solution)/shard_map/while/body/eval_jaxpr/ppermute | solution.py:15
  169.3 46.0 %reduce-scatter.3.cloned.1.call-start = ((), (), s32[]{:S(2)}) async-start(), calls=%async_computation.2 | async-start | bytes 655360 | tf_op jit(solution)/shard_map/while/body/eval_jaxpr/reduce_scatter | solution.py:54
  190.0 91.5 %reduce-scatter.5.cloned.1.call-start = ((), (), s32[]{:S(2)}) async-start(), calls=%async_computation.3 | async-start | bytes 655360 | tf_op jit(solution)/shard_map/while/body/eval_jaxpr/reduce_scatter | solution.py:54
  216.3 87.4 %copy-start.3 = (bf16[64,256]{1,0:T(8,128)(2,1)}, bf16[64,256]{1,0:T(8,128)(2,1)S(1)}, u32[]{:S(2)}) copy-start(bf16[64,256]{1,0:T(8,128)(2,1)S(1)} %get-tuple-element.345) | copy-start | bytes 98308 | tf_op jit(solution)/shard_map/while
  216.3 5.2 %collective-permute-start = (bf16[64,256]{1,0:T(8,128)(2,1)S(1)}, bf16[64,256]{1,0:T(8,128)(2,1)S(1)}, u32[]{:S(2)}, u32[]{:S(2)}) collective-permute-start(bf16[64,256]{1,0:T(8,128)(2,1)S(1)} %get-tuple-element.345), channel_id=1, source_target_pairs={{0,4},{4,8},{8,12},{12,16},{16,20},{20,24},{24,28},{28,0},{1,5},{5... | collective-permute-start | bytes 98312 | tf_op jit(solution)/shard_map/while/body/eval_jaxpr/ppermute | solution.py:13
  221.5 5.5 %collective-permute-start.1 = (bf16[64,256]{1,0:T(8,128)(2,1)S(1)}, bf16[64,256]{1,0:T(8,128)(2,1)S(1)}, u32[]{:S(2)}, u32[]{:S(2)}) collective-permute-start(bf16[64,256]{1,0:T(8,128)(2,1)S(1)} %collective-permute-done), channel_id=1, source_target_pairs={{0,4},{4,8},{8,12},{12,16},{16,20},{20,24},{24,28},{28,0},{1,5},{5... | collective-permute-start | bytes 98312 | tf_op jit(solution)/shard_map/while/body/eval_jaxpr/ppermute | solution.py:13
  221.5 5.5 %collective-permute-start.4 = (bf16[64,256]{1,0:T(8,128)(2,1)S(1)}, bf16[64,256]{1,0:T(8,128)(2,1)S(1)}, u32[]{:S(2)}, u32[]{:S(2)}) collective-permute-start(bf16[64,256]{1,0:T(8,128)(2,1)S(1)} %get-tuple-element.345), channel_id=1, source_target_pairs={{0,28},{4,0},{8,4},{12,8},{16,12},{20,16},{24,20},{28,24},{1,29},{... | collective-permute-start | bytes 98312 | tf_op jit(solution)/shard_map/while/body/eval_jaxpr/ppermute | solution.py:15
  227.0 5.1 %collective-permute-start.2 = (bf16[64,256]{1,0:T(8,128)(2,1)S(1)}, bf16[64,256]{1,0:T(8,128)(2,1)S(1)}, u32[]{:S(2)}, u32[]{:S(2)}) collective-permute-start(bf16[64,256]{1,0:T(8,128)(2,1)S(1)} %collective-permute-done.1), channel_id=1, source_target_pairs={{0,4},{4,8},{8,12},{12,16},{16,20},{20,24},{24,28},{28,0},{1,5},{5... | collective-permute-start | bytes 98312 | tf_op jit(solution)/shard_map/while/body/eval_jaxpr/ppermute | solution.py:13
  227.0 13.9 %collective-permute-start.5 = (bf16[64,256]{1,0:T(8,128)(2,1)S(1)}, bf16[64,256]{1,0:T(8,128)(2,1)S(1)}, u32[]{:S(2)}, u32[]{:S(2)}) collective-permute-start(bf16[64,256]{1,0:T(8,128)(2,1)S(1)} %collective-permute-done.4), channel_id=1, source_target_pairs={{0,28},{4,0},{8,4},{12,8},{16,12},{20,16},{24,20},{28,24},{1,29},{... | collective-permute-start | bytes 98312 | tf_op jit(solution)/shard_map/while/body/eval_jaxpr/ppermute | solution.py:15
  232.1 12.4 %collective-permute-start.3 = (bf16[64,256]{1,0:T(8,128)(2,1)S(1)}, bf16[64,256]{1,0:T(8,128)(2,1)S(1)}, u32[]{:S(2)}, u32[]{:S(2)}) collective-permute-start(bf16[64,256]{1,0:T(8,128)(2,1)S(1)} %collective-permute-done.2), channel_id=1, source_target_pairs={{0,4},{4,8},{8,12},{12,16},{16,20},{20,24},{24,28},{28,0},{1,5},{5... | collective-permute-start | bytes 98312 | tf_op jit(solution)/shard_map/while/body/eval_jaxpr/ppermute | solution.py:13
  240.9 5.2 %collective-permute-start.6 = (bf16[64,256]{1,0:T(8,128)(2,1)S(1)}, bf16[64,256]{1,0:T(8,128)(2,1)S(1)}, u32[]{:S(2)}, u32[]{:S(2)}) collective-permute-start(bf16[64,256]{1,0:T(8,128)(2,1)S(1)} %collective-permute-done.5), channel_id=1, source_target_pairs={{0,28},{4,0},{8,4},{12,8},{16,12},{20,16},{24,20},{28,24},{1,29},{... | collective-permute-start | bytes 98312 | tf_op jit(solution)/shard_map/while/body/eval_jaxpr/ppermute | solution.py:15
  282.5 21.3 %copy-start.1 = (bf16[64,256]{1,0:T(8,128)(2,1)}, bf16[64,256]{1,0:T(8,128)(2,1)S(1)}, u32[]{:S(2)}) copy-start(bf16[64,256]{1,0:T(8,128)(2,1)S(1)} %get-tuple-element.346) | copy-start | bytes 98308 | tf_op jit(solution)/shard_map/while
  282.5 5.2 %collective-permute-start.7 = (bf16[64,256]{1,0:T(8,128)(2,1)S(1)}, bf16[64,256]{1,0:T(8,128)(2,1)S(1)}, u32[]{:S(2)}, u32[]{:S(2)}) collective-permute-start(bf16[64,256]{1,0:T(8,128)(2,1)S(1)} %get-tuple-element.346), channel_id=1, source_target_pairs={{0,4},{4,8},{8,12},{12,16},{16,20},{20,24},{24,28},{28,0},{1,5},{5... | collective-permute-start | bytes 98312 | tf_op jit(solution)/shard_map/while/body/eval_jaxpr/ppermute | solution.py:13
  287.7 5.4 %collective-permute-start.8 = (bf16[64,256]{1,0:T(8,128)(2,1)S(1)}, bf16[64,256]{1,0:T(8,128)(2,1)S(1)}, u32[]{:S(2)}, u32[]{:S(2)}) collective-permute-start(bf16[64,256]{1,0:T(8,128)(2,1)S(1)} %collective-permute-done.7), channel_id=1, source_target_pairs={{0,4},{4,8},{8,12},{12,16},{16,20},{20,24},{24,28},{28,0},{1,5},{5... | collective-permute-start | bytes 98312 | tf_op jit(solution)/shard_map/while/body/eval_jaxpr/ppermute | solution.py:13
  287.7 5.4 %collective-permute-start.11 = (bf16[64,256]{1,0:T(8,128)(2,1)S(1)}, bf16[64,256]{1,0:T(8,128)(2,1)S(1)}, u32[]{:S(2)}, u32[]{:S(2)}) collective-permute-start(bf16[64,256]{1,0:T(8,128)(2,1)S(1)} %get-tuple-element.346), channel_id=1, source_target_pairs={{0,28},{4,0},{8,4},{12,8},{16,12},{20,16},{24,20},{28,24},{1,29},{... | collective-permute-start | bytes 98312 | tf_op jit(solution)/shard_map/while/body/eval_jaxpr/ppermute | solution.py:15
  293.1 5.2 %collective-permute-start.9 = (bf16[64,256]{1,0:T(8,128)(2,1)S(1)}, bf16[64,256]{1,0:T(8,128)(2,1)S(1)}, u32[]{:S(2)}, u32[]{:S(2)}) collective-permute-start(bf16[64,256]{1,0:T(8,128)(2,1)S(1)} %collective-permute-done.8), channel_id=1, source_target_pairs={{0,4},{4,8},{8,12},{12,16},{16,20},{20,24},{24,28},{28,0},{1,5},{5... | collective-permute-start | bytes 98312 | tf_op jit(solution)/shard_map/while/body/eval_jaxpr/ppermute | solution.py:13
  293.1 5.2 %collective-permute-start.12 = (bf16[64,256]{1,0:T(8,128)(2,1)S(1)}, bf16[64,256]{1,0:T(8,128)(2,1)S(1)}, u32[]{:S(2)}, u32[]{:S(2)}) collective-permute-start(bf16[64,256]{1,0:T(8,128)(2,1)S(1)} %collective-permute-done.11), channel_id=1, source_target_pairs={{0,28},{4,0},{8,4},{12,8},{16,12},{20,16},{24,20},{28,24},{1,29},{... | collective-permute-start | bytes 98312 | tf_op jit(solution)/shard_map/while/body/eval_jaxpr/ppermute | solution.py:15
  298.4 5.1 %collective-permute-start.10 = (bf16[64,256]{1,0:T(8,128)(2,1)S(1)}, bf16[64,256]{1,0:T(8,128)(2,1)S(1)}, u32[]{:S(2)}, u32[]{:S(2)}) collective-permute-start(bf16[64,256]{1,0:T(8,128)(2,1)S(1)} %collective-permute-done.9), channel_id=1, source_target_pairs={{0,4},{4,8},{8,12},{12,16},{16,20},{20,24},{24,28},{28,0},{1,5},{5... | collective-permute-start | bytes 98312 | tf_op jit(solution)/shard_map/while/body/eval_jaxpr/ppermute | solution.py:13
  298.4 5.2 %collective-permute-start.13 = (bf16[64,256]{1,0:T(8,128)(2,1)S(1)}, bf16[64,256]{1,0:T(8,128)(2,1)S(1)}, u32[]{:S(2)}, u32[]{:S(2)}) collective-permute-start(bf16[64,256]{1,0:T(8,128)(2,1)S(1)} %collective-permute-done.12), channel_id=1, source_target_pairs={{0,28},{4,0},{8,4},{12,8},{16,12},{20,16},{24,20},{28,24},{1,29},{... | collective-permute-start | bytes 98312 | tf_op jit(solution)/shard_map/while/body/eval_jaxpr/ppermute | solution.py:15
  303.8 2.1 copy-start.4
Sparse Core Ops, SparseCore 0:
  56.9 23.8 reduce-scatter.2
  121.6 25.3 reduce-scatter.4
  190.1 25.1 reduce-scatter.2
  256.1 25.3 reduce-scatter.4
